TPU v7x, 32 devices: a whole 2x2x4 slice. The times are simulated.
32 devices in a mesh: exp: 8 (over z, x), tp: 4 (over y, core).
Axes of the slice: x: 2, y: 2, z: 4, core: 2. Of those that a mesh axis runs over, the one named last changes fastest.
Arguments:
- tokens: bfloat16 [4096, 2048], P(('exp', 'tp')), may hold values from -6 to 6
- cotangent: bfloat16 [4096, 2048], P(('exp', 'tp')), may hold values from -6 to 6
- attention_gain: float32 [2048], replicated, may hold values from 0.5 to 1.5
- query_weight: bfloat16 [2048, 2048], P(None, 'tp'), may hold values from -0.125 to 0.125
- key_weight: bfloat16 [2048, 2048], P(None, 'tp'), may hold values from -0.125 to 0.125
- value_weight: bfloat16 [2048, 2048], P(None, 'tp'), may hold values from -0.125 to 0.125
- output_weight: bfloat16 [2048, 2048], P('tp'), may hold values from -1 to 1
- query_norm: float32 [2048], P('tp'), may hold values from 0.5 to 1.5
- key_norm: float32 [2048], P('tp'), may hold values from 0.5 to 1.5
- mixture_gain: float32 [2048], replicated, may hold values from 0.5 to 1.5
- router_weight: bfloat16 [2048, 16], replicated, may hold values from -0.0625 to 0.0625
- gate_weight: bfloat16 [16, 2048, 1024], P('exp', None, 'tp'), may hold values from -0.125 to 0.125
- up_weight: bfloat16 [16, 2048, 1024], P('exp', None, 'tp'), may hold values from -0.125 to 0.125
- down_weight: bfloat16 [16, 1024, 2048], P('exp', 'tp'), may hold values from -3 to 3
- routes: int32 [4096, 8], P(('exp', 'tp')), may hold values from 0 to 15, all different within a row
- segments: int32 [8, 512], P('exp'), may hold values from 0 to 3, never falling along the last dimension, each value on 1 to 256 neighbouring positions
Outputs:
- output: bfloat16 [4096, 2048], P(('exp', 'tp'))
- tokens_grad: float32 [4096, 2048], P(('exp', 'tp'))
- attention_gain_grad: float32 [2048], replicated
- query_weight_grad: float32 [2048, 2048], P(None, 'tp')
- key_weight_grad: float32 [2048, 2048], P(None, 'tp')
- value_weight_grad: float32 [2048, 2048], P(None, 'tp')
- output_weight_grad: float32 [2048, 2048], P('tp')
- query_norm_grad: float32 [2048], P('tp')
- key_norm_grad: float32 [2048], P('tp')
- mixture_gain_grad: float32 [2048], replicated
- router_weight_grad: float32 [2048, 16], replicated
- gate_weight_grad: float32 [16, 2048, 1024], P('exp', None, 'tp')
- up_weight_grad: float32 [16, 2048, 1024], P('exp', None, 'tp')
- down_weight_grad: float32 [16, 1024, 2048], P('exp', 'tp')
Inputs may be any that keep to these rules, and one draw needn't show every extreme that they name: `routes`: each token names 8 different experts; every expert is named by some token. `segments`: in each row the ids never fall and start at 0; each of the 4 ids covers 1 to 256 consecutive positions, one exactly 256.
All inputs are finite; a program needn't handle non-finite values.
Results may differ from a plain program's by a relative error of at most 0.025.
Values may be sent and summed in bfloat16 or wider, within the bound.
No kernel may reach another device: no remote copies, remote signals or barrier semaphores. Data moves between devices by JAX's collectives and lax.ppermute only.
A program may use at most 256 MiB of HBM per device.

v0:
```python
import math
import jax
import jax.numpy as jnp
from jax import lax
from jax.sharding import PartitionSpec as P

HD = 128
EPS = 1e-05
HIGH = lax.Precision.HIGHEST


def inverse_rms(values):
    return lax.rsqrt(jnp.mean(values * values, axis=-1, keepdims=True) + EPS)


def norm_backward(grad_normed, normalized_input, factor):
    return factor * (
        grad_normed
        - normalized_input * jnp.mean(grad_normed * normalized_input, axis=-1, keepdims=True)
    )


def contract_rows(first_arg, second_arg):
    return lax.dot_general(
        first_arg, second_arg, (((0,), (0,)), ((), ())), preferred_element_type=jnp.float32
    )


def contract_cols(first_arg, second_arg):
    return lax.dot_general(
        first_arg, second_arg, (((1,), (1,)), ((), ())), preferred_element_type=jnp.float32
    )


def positions_of(segment_row):
    earlier = jnp.sum((segment_row[None, :] < segment_row[:, None]).astype(jnp.int32), axis=1)
    return jnp.arange(segment_row.shape[0], dtype=jnp.int32) - earlier


def rope_tables(positions, head_size):
    half_dim = head_size // 2
    inverse_freq = 10000.0 ** (-2.0 * jnp.arange(half_dim).astype(jnp.float32) / head_size)
    angles = positions.astype(jnp.float32)[:, None] * inverse_freq[None, :]
    return (jnp.cos(angles)[:, None, :], jnp.sin(angles)[:, None, :])


def rotate(values, cos_table, sin_table):
    half_dim = values.shape[-1] // 2
    first_half = values[..., :half_dim]
    second_half = values[..., half_dim:]
    return jnp.concatenate(
        [
            first_half * cos_table - second_half * sin_table,
            second_half * cos_table + first_half * sin_table,
        ],
        axis=-1,
    )


def gather_expert_rows(local_rows):
    return lax.all_gather(local_rows, "tp", axis=1, tiled=True)


def body(
    tokens,
    cotangent,
    attention_gain,
    query_weight,
    key_weight,
    value_weight,
    output_weight,
    query_norm,
    key_norm,
    mixture_gain,
    router_weight,
    gate_weight,
    up_weight,
    down_weight,
    routes,
    segments,
):
    tok_rows, model_width = tokens.shape
    top_count = routes.shape[1]
    experts_all = router_weight.shape[1]
    capacity = tok_rows * top_count * 7 // (8 * experts_all)
    local_width = query_weight.shape[1]
    head_count = local_width // HD
    inv_sqrt = 1.0 / math.sqrt(HD)
    inputs = tokens.astype(jnp.float32)
    scale_one = inverse_rms(inputs)
    normed_one = inputs * scale_one
    attention_in = (normed_one * attention_gain).astype(jnp.bfloat16)
    gathered_rows = lax.all_gather(attention_in, "tp", axis=0, tiled=True)
    row_length = gathered_rows.shape[0]
    queries = jnp.dot(gathered_rows, query_weight, preferred_element_type=jnp.float32).reshape(
        row_length, head_count, HD
    )
    key_rows = jnp.dot(gathered_rows, key_weight, preferred_element_type=jnp.float32).reshape(
        row_length, head_count, HD
    )
    value_rows = (
        jnp.dot(gathered_rows, value_weight, preferred_element_type=jnp.float32)
        .astype(jnp.bfloat16)
        .reshape(row_length, head_count, HD)
    )
    query_gain = query_norm.reshape(head_count, HD)
    key_gain = key_norm.reshape(head_count, HD)
    query_scale = inverse_rms(queries)
    query_hat = queries * query_scale
    key_scale = inverse_rms(key_rows)
    key_hat = key_rows * key_scale
    segment_row = segments[0]
    cos_table, sin_table = rope_tables(positions_of(segment_row), HD)
    query_rot = rotate(query_hat * query_gain, cos_table, sin_table).astype(jnp.bfloat16)
    key_rot = rotate(key_hat * key_gain, cos_table, sin_table).astype(jnp.bfloat16)
    block_rows = min(512, row_length)
    position = jnp.arange(row_length, dtype=jnp.int32)

    def block_scores(first_row):
        scores = (
            jnp.einsum("ihd,jhd->hij", query_rot, key_rot, preferred_element_type=jnp.float32)
            * inv_sqrt
        )
        allowed = (
            segment_row[first_row : first_row + block_rows, None] == segment_row[None, :]
        ) & (position[None, :] <= position[first_row : first_row + block_rows, None])
        return jnp.where(allowed[None], scores, -1e30)

    first_row = 0
    scores = block_scores(first_row)
    row_peak = jnp.max(scores, axis=-1, keepdims=True)
    shifted = jnp.exp(scores - row_peak)
    denominator = jnp.sum(shifted, axis=-1, keepdims=True)
    weights = (shifted / denominator).astype(jnp.bfloat16)
    log_totals = [row_peak + jnp.log(denominator)]
    attended_parts = jnp.einsum(
        "hij,jhd->ihd", weights, value_rows, preferred_element_type=jnp.float32
    ).reshape(block_rows, local_width)
    attended = attended_parts.astype(jnp.bfloat16)
    attention_block = lax.psum_scatter(
        jnp.dot(attended, output_weight, preferred_element_type=jnp.float32).astype(jnp.bfloat16),
        "tp",
        scatter_dimension=0,
        tiled=True,
    ).astype(jnp.float32)
    middle = inputs + attention_block
    scale_two = inverse_rms(middle)
    normed_two = middle * scale_two
    mixture_in = (normed_two * mixture_gain).astype(jnp.bfloat16)
    logits = jnp.dot(mixture_in, router_weight, preferred_element_type=jnp.float32)
    probabilities = jax.nn.softmax(logits, axis=-1)
    expert_ids = jnp.arange(experts_all, dtype=jnp.int32)
    chosen = (routes[:, :, None] == expert_ids[None, None, :]).astype(jnp.float32)
    gate_values = jnp.sum(chosen * probabilities[:, None, :], axis=-1)
    assigned = routes.reshape(-1)
    matches = (assigned[:, None] == expert_ids[None, :]).astype(jnp.int32)
    earlier = jnp.sum(jnp.cumsum(matches, axis=0) * matches, axis=1) - 1
    slot_ids = jnp.where(earlier < capacity, assigned * capacity + earlier, experts_all * capacity)
    assign_count = tok_rows * top_count
    owners = (
        jnp.full((experts_all * capacity + 1,), assign_count, jnp.int32)
        .at[slot_ids]
        .set(jnp.arange(assign_count, dtype=jnp.int32))[:-1]
    )
    source_rows = owners // top_count
    input_pad = jnp.concatenate([mixture_in, jnp.zeros((1, model_width), jnp.bfloat16)], axis=0)
    outgoing = input_pad[source_rows].reshape(experts_all, capacity, model_width)
    arrived = lax.all_to_all(outgoing, "exp", split_axis=0, concat_axis=1, tiled=True)
    expert_in = gather_expert_rows(arrived)
    gate_pre = jnp.einsum(
        "erd,edf->erf", expert_in, gate_weight, preferred_element_type=jnp.float32
    )
    up_pre = jnp.einsum("erd,edf->erf", expert_in, up_weight, preferred_element_type=jnp.float32)
    hidden = (jax.nn.silu(gate_pre) * up_pre).astype(jnp.bfloat16)
    partial_out = jnp.einsum(
        "erf,efd->erd", hidden, down_weight, preferred_element_type=jnp.float32
    )
    returned = lax.psum_scatter(
        partial_out.astype(jnp.bfloat16), "tp", scatter_dimension=1, tiled=True
    )
    combined = lax.all_to_all(returned, "exp", split_axis=1, concat_axis=0, tiled=True)
    output_pad = jnp.concatenate(
        [combined.reshape(-1, model_width), jnp.zeros((1, model_width), jnp.bfloat16)], axis=0
    )
    expert_out = output_pad[slot_ids].astype(jnp.float32).reshape(tok_rows, top_count, model_width)
    mixture = jnp.sum(gate_values[:, :, None] * expert_out, axis=1)
    output = (middle + mixture).astype(jnp.bfloat16)
    grad_out = cotangent.astype(jnp.float32)
    grad_gate = jnp.sum(grad_out[:, None, :] * expert_out, axis=-1)
    grad_sent = (
        (gate_values[:, :, None] * grad_out[:, None, :])
        .reshape(assign_count, model_width)
        .astype(jnp.bfloat16)
    )
    grad_pad = jnp.concatenate([grad_sent, jnp.zeros((1, model_width), jnp.bfloat16)], axis=0)
    grad_outgoing = grad_pad[owners].reshape(experts_all, capacity, model_width)
    grad_arrived = lax.all_to_all(grad_outgoing, "exp", split_axis=0, concat_axis=1, tiled=True)
    grad_expert = lax.all_gather(grad_arrived, "tp", axis=1, tiled=True)
    gate_pre = jnp.einsum(
        "erd,edf->erf", expert_in, gate_weight, preferred_element_type=jnp.float32
    )
    up_pre = jnp.einsum("erd,edf->erf", expert_in, up_weight, preferred_element_type=jnp.float32)
    gate_sig = jax.nn.sigmoid(gate_pre)
    gate_act = gate_pre * gate_sig
    hidden = (gate_act * up_pre).astype(jnp.bfloat16)
    grad_hidden = jnp.einsum(
        "erd,efd->erf", grad_expert, down_weight, preferred_element_type=jnp.float32
    )
    down_grad = jnp.einsum("erf,erd->efd", hidden, grad_expert, preferred_element_type=jnp.float32)
    grad_gate_pre = (grad_hidden * up_pre * gate_sig * (1.0 + gate_pre * (1.0 - gate_sig))).astype(
        jnp.bfloat16
    )
    grad_up_pre = (grad_hidden * gate_act).astype(jnp.bfloat16)
    gate_grad = jnp.einsum(
        "erd,erf->edf", expert_in, grad_gate_pre, preferred_element_type=jnp.float32
    )
    up_grad = jnp.einsum("erd,erf->edf", expert_in, grad_up_pre, preferred_element_type=jnp.float32)
    grad_in_part = jnp.einsum(
        "erf,edf->erd", grad_gate_pre, gate_weight, preferred_element_type=jnp.float32
    ) + jnp.einsum("erf,edf->erd", grad_up_pre, up_weight, preferred_element_type=jnp.float32)
    grad_in = lax.psum_scatter(
        grad_in_part.astype(jnp.bfloat16), "tp", scatter_dimension=1, tiled=True
    )
    grad_home = lax.all_to_all(grad_in, "exp", split_axis=1, concat_axis=0, tiled=True)
    home_pad = jnp.concatenate(
        [grad_home.reshape(-1, model_width), jnp.zeros((1, model_width), jnp.bfloat16)], axis=0
    )
    grad_assigned = home_pad[slot_ids].astype(jnp.float32).reshape(tok_rows, top_count, model_width)
    grad_probs = jnp.sum(chosen * grad_gate[:, :, None], axis=1)
    grad_logits = probabilities * (
        grad_probs - jnp.sum(grad_probs * probabilities, axis=-1, keepdims=True)
    )
    router_grad = jnp.dot(mixture_in.astype(jnp.float32).T, grad_logits, precision=HIGH)
    grad_mixture_in = jnp.sum(grad_assigned, axis=1) + jnp.dot(
        grad_logits, router_weight.astype(jnp.float32).T, precision=HIGH
    )
    mixture_gain_grad = jnp.sum(grad_mixture_in * normed_two, axis=0)
    grad_middle = grad_out + norm_backward(grad_mixture_in * mixture_gain, normed_two, scale_two)
    grad_attention = grad_middle.astype(jnp.bfloat16)
    row_grad = lax.all_gather(grad_attention, "tp", axis=0, tiled=True)
    output_weight_grad = contract_rows(attended, row_grad)
    grad_attended = contract_cols(row_grad, output_weight).astype(jnp.bfloat16)
    grad_query_parts = []
    grad_key_rows = jnp.zeros((row_length, head_count, HD), jnp.float32)
    grad_value_rows = jnp.zeros((row_length, head_count, HD), jnp.float32)
    for block_index, first_row in enumerate(range(0, row_length, block_rows)):
        scores = block_scores(first_row)
        probs_block = jnp.exp(scores - log_totals[block_index])
        weights = probs_block.astype(jnp.bfloat16)
        grad_block = grad_attended.reshape(block_rows, head_count, HD)
        grad_weights = jnp.einsum(
            "ihd,jhd->hij", grad_block, value_rows, preferred_element_type=jnp.float32
        )
        inner_sum = jnp.sum(grad_weights * probs_block, axis=-1, keepdims=True)
        grad_scores = (probs_block * (grad_weights - inner_sum)).astype(jnp.bfloat16)
        grad_query_parts.append(
            jnp.einsum("hij,jhd->ihd", grad_scores, key_rot, preferred_element_type=jnp.float32)
            * inv_sqrt
        )
        grad_key_rows = (
            jnp.einsum("hij,ihd->jhd", grad_scores, query_rot, preferred_element_type=jnp.float32)
            * inv_sqrt
        )
        grad_value_rows = jnp.einsum(
            "hij,ihd->jhd", weights, grad_block, preferred_element_type=jnp.float32
        )
    grad_query_norm = rotate(grad_query_parts[0], cos_table, -sin_table)
    grad_key_norm = rotate(grad_key_rows, cos_table, -sin_table)
    query_norm_grad = jnp.sum(grad_query_norm * query_hat, axis=0).reshape(local_width)
    key_norm_grad = jnp.sum(grad_key_norm * key_hat, axis=0).reshape(local_width)
    grad_queries = (
        norm_backward(grad_query_norm * query_gain, query_hat, query_scale)
        .reshape(row_length, local_width)
        .astype(jnp.bfloat16)
    )
    grad_keys = (
        norm_backward(grad_key_norm * key_gain, key_hat, key_scale)
        .reshape(row_length, local_width)
        .astype(jnp.bfloat16)
    )
    grad_values = grad_value_rows.reshape(row_length, local_width).astype(jnp.bfloat16)
    query_weight_grad = contract_rows(gathered_rows, grad_queries)
    key_weight_grad = contract_rows(gathered_rows, grad_keys)
    value_weight_grad = contract_rows(gathered_rows, grad_values)
    total_grad = contract_cols(grad_queries, query_weight)
    total_grad = total_grad + contract_cols(grad_keys, key_weight)
    grad_attention_in = lax.psum_scatter(
        (total_grad + contract_cols(grad_values, value_weight)).astype(jnp.bfloat16),
        "tp",
        scatter_dimension=0,
        tiled=True,
    ).astype(jnp.float32)
    attention_gain_grad = jnp.sum(grad_attention_in * normed_one, axis=0)
    tokens_grad = grad_middle + norm_backward(
        grad_attention_in * attention_gain, normed_one, scale_one
    )
    head_sums = (
        lax.psum(query_weight_grad.astype(jnp.bfloat16), "exp").astype(jnp.float32),
        lax.psum(key_weight_grad.astype(jnp.bfloat16), "exp").astype(jnp.float32),
        lax.psum(value_weight_grad.astype(jnp.bfloat16), "exp").astype(jnp.float32),
        lax.psum(output_weight_grad.astype(jnp.bfloat16), "exp").astype(jnp.float32),
        lax.psum(query_norm_grad.astype(jnp.bfloat16), "exp").astype(jnp.float32),
        lax.psum(key_norm_grad.astype(jnp.bfloat16), "exp").astype(jnp.float32),
    )
    shared_sums = lax.psum((attention_gain_grad, mixture_gain_grad, router_grad), ("exp", "tp"))
    return (
        output,
        tokens_grad,
        shared_sums[0],
        head_sums[0],
        head_sums[1],
        head_sums[2],
        head_sums[3],
        head_sums[4],
        head_sums[5],
        shared_sums[1],
        shared_sums[2],
        gate_grad,
        up_grad,
        down_grad,
    )


def solution(mesh):
    return jax.shard_map(
        body,
        mesh=mesh,
        in_specs=(
            P(("exp", "tp"), None),
            P(("exp", "tp"), None),
            P(),
            P(None, "tp"),
            P(None, "tp"),
            P(None, "tp"),
            P("tp", None),
            P("tp"),
            P("tp"),
            P(),
            P(),
            P("exp", None, "tp"),
            P("exp", None, "tp"),
            P("exp", "tp", None),
            P(("exp", "tp"), None),
            P("exp", None),
        ),
        out_specs=(
            P(("exp", "tp"), None),
            P(("exp", "tp"), None),
            P(),
            P(None, "tp"),
            P(None, "tp"),
            P(None, "tp"),
            P("tp", None),
            P("tp"),
            P("tp"),
            P(),
            P(),
            P("exp", None, "tp"),
            P("exp", None, "tp"),
            P("exp", "tp", None),
        ),
        check_vma=False,
    )
```

profile of v0, /device:TPU:0, one launch (start us, length us, event | category | flops | bytes accessed | tf_op | source)
XLA Modules:
  0.0 1259.1 jit_solution(2690776216427497176)
XLA Ops:
  15.7 21.0 %all-gather.5.cloned.1.call-done = bf16[512,2048]{1,0:T(8,128)(2,1)} async-done(((bf16[128,2048]{1,0:T(8,128)(2,1)}), bf16[512,2048]{1,0:T(8,128)(2,1)}) %all-gather.5.cloned.1.call-update) | async-done | bytes 2097168 | tf_op jit(solution)/shard_map/all_gather | solution.py:93
  36.7 3.5 multiply_reduce_fusion.6
  41.6 4.5 multiply_reduce_fusion.7
  62.5 4.5 reduce-window.6
  67.5 4.3 scatter_custom_fusion
  71.9 21.5 %reduce-scatter.5.cloned.1.call-done = bf16[128,2048]{1,0:T(8,128)(2,1)} async-done(((bf16[512,2048]{1,0:T(8,128)(2,1)}), bf16[128,2048]{1,0:T(8,128)(2,1)}) %reduce-scatter.5.cloned.1.call-update) | async-done | bytes 524304 | tf_op jit(solution)/shard_map/reduce_scatter | solution.py:140
  96.8 5.0 gather_fusion
  101.7 87.5 %all_to_all.66 = bf16[16,56,2048]{2,1,0:T(8,128)(2,1)S(1)} all-to-all(bf16[16,56,2048]{2,1,0:T(8,128)(2,1)} %bitcast.163), channel_id=1, replica_groups=mesh['exp'=8,'tp'=4] {'exp'}, dimensions={0} | all-to-all | bytes 7340032 | tf_op jit(solution)/shard_map/all_to_all | solution.py:168
  197.7 12.3 gather_fusion.2
  210.0 85.0 %all_to_all.67 = bf16[16,56,2048]{2,1,0:T(8,128)(2,1)S(1)} all-to-all(bf16[16,56,2048]{2,1,0:T(8,128)(2,1)} %bitcast.164), channel_id=1, replica_groups=mesh['exp'=8,'tp'=4] {'exp'}, dimensions={0} | all-to-all | bytes 7340032 | tf_op jit(solution)/shard_map/all_to_all | solution.py:197
  297.5 13.5 %fusion.53 = f32[2,1792,256]{2,1,0:T(8,128)} fusion(bf16[2,1792,2048]{2,1,0:T(8,128)(2,1)} %all-gather.7.cloned.1.call-done, bf16[2,2048,256]{2,1,0:T(8,128)(2,1)} %param.28), kind=kOutput, calls=%fused_computation.159 | convolution fusion | flops 3758096384 | bytes 20447232 | tf_op jit(solution)/shard_map/erd,edf->erf/dot_general | solution.py:173
  310.9 9.8 fusion.52
  320.8 68.7 %all-gather.9.cloned.1.call-done = bf16[2,1792,2048]{2,1,0:T(8,128)(2,1)} async-done(((bf16[2,448,2048]{2,1,0:T(8,128)(2,1)}), bf16[2,1792,2048]{2,1,0:T(8,128)(2,1)}) %all-gather.9.cloned.1.call-update) | async-done | bytes 14680080 | tf_op jit(solution)/shard_map/all_gather | solution.py:198
  389.5 15.6 %multiply_convert_fusion.1 = (bf16[2,1792,256]{2,1,0:T(8,128)(2,1)}, bf16[2,1792,256]{2,1,0:T(8,128)(2,1)}, bf16[2,1792,256]{2,1,0:T(8,128)(2,1)}) fusion(f32[2,1792,256]{2,1,0:T(8,128)} %fusion.52, f32[2,1792,256]{2,1,0:T(8,128)} %fusion.53, bf16[2,1792,2048]{2,1,0:T(8,128)(2,1)} %all-gather.9.cloned.1.call-done, bf16[2,256,2048]{2,1,0:T(8,128)(2,1)S(1)} %copy-done), kind=kOutput, calls=%fused_computation.22 | convolution fusion | flops 3771858944 | bytes 29622272 | tf_op jit(solution)/shard_map/erd,efd->erf/dot_general | solution.py:206
  405.0 8.7 convolution_convert_fusion
  415.3 19.2 %fusion.54 = f32[2,1792,2048]{2,1,0:T(8,128)} fusion(bf16[2,1792,256]{2,1,0:T(8,128)(2,1)} %get-tuple-element.33, bf16[2,2048,256]{2,1,0:T(8,128)(2,1)S(1)} %copy-done.34), kind=kOutput, calls=%fused_computation.160 | convolution fusion | flops 3758096384 | bytes 33292288 | tf_op jit(solution)/shard_map/erf,edf->erd/dot_general | solution.py:218
  434.6 17.7 %add_convert_fusion = bf16[2,1792,2048]{2,1,0:T(8,128)(2,1)} fusion(f32[2,1792,2048]{2,1,0:T(8,128)} %fusion.54, bf16[2,1792,256]{2,1,0:T(8,128)(2,1)S(1)} %copy-done.43, bf16[2,2048,256]{2,1,0:T(8,128)(2,1)S(1)} %copy-done.35), kind=kOutput, calls=%fused_computation.5 | convolution fusion | flops 3772776448 | bytes 47972352 | tf_op jit(solution)/shard_map/erf,edf->erd/dot_general | solution.py:220
  452.3 74.5 %reduce-scatter.7.cloned.1.call-done = bf16[2,448,2048]{2,1,0:T(8,128)(2,1)} async-done(((bf16[2,1792,2048]{2,1,0:T(8,128)(2,1)}), bf16[2,448,2048]{2,1,0:T(8,128)(2,1)}) %reduce-scatter.7.cloned.1.call-update) | async-done | bytes 3670032 | tf_op jit(solution)/shard_map/reduce_scatter | solution.py:178
  526.8 7.6 copy.151
  534.4 5.5 all-to-all-start.1
  539.9 102.3 %reduce-scatter.9.cloned.1.call-done = bf16[2,448,2048]{2,1,0:T(8,128)(2,1)} async-done(((bf16[2,1792,2048]{2,1,0:T(8,128)(2,1)}), bf16[2,448,2048]{2,1,0:T(8,128)(2,1)}) %reduce-scatter.9.cloned.1.call-update) | async-done | bytes 3670032 | tf_op jit(solution)/shard_map/reduce_scatter | solution.py:221
  642.3 7.6 copy.155
  649.9 5.5 all-to-all-start.3
  655.9 3.7 copy.152
  661.9 11.3 gather_fusion.1
  673.2 5.8 fusion.1
  679.2 58.3 %all-to-all-done.3 = bf16[2,448,2048]{2,0,1:T(2,128)(2,1)} async-done(((bf16[2,448,2048]{2,0,1:T(2,128)(2,1)}), bf16[2,448,2048]{2,0,1:T(2,128)(2,1)}, u32[]{:S(2)}, u32[]{:S(2)}) %all-to-all-start.3) | async-done | bytes 3670048 | tf_op jit(solution)/shard_map/all_to_all | solution.py:224
  737.5 3.7 copy.156
  743.4 11.3 gather_fusion.3
  754.8 5.2 convert_reduce_fusion
  762.6 20.6 %all-gather.11.cloned.1.call-done = bf16[512,2048]{1,0:T(8,128)(2,1)} async-done(((bf16[128,2048]{1,0:T(8,128)(2,1)}), bf16[512,2048]{1,0:T(8,128)(2,1)}) %all-gather.11.cloned.1.call-update) | async-done | bytes 2097168 | tf_op jit(solution)/shard_map/all_gather | solution.py:240
  783.2 3.6 convolution_convert_fusion.6
  804.2 3.1 fusion.55
  809.7 2.7 add_convert_fusion.1
  812.5 4.4 convolution_convert_fusion.1
  816.9 2.6 convolution_convert_fusion.2
  819.5 2.6 convolution_convert_fusion.3
  822.2 2.6 convolution_convert_fusion.4
  824.9 11.0 fusion.58
  835.9 11.0 fusion.57
  847.0 5.7 fusion.59
  853.7 22.3 %all-reduce.5 = (bf16[512]{0:T(512)(128)(2,1)S(1)}, bf16[512]{0:T(512)(128)(2,1)S(1)}) all-reduce(bf16[512]{0:T(512)(128)(2,1)S(1)} %get-tuple-element.37, bf16[512]{0:T(512)(128)(2,1)S(1)} %get-tuple-element.35), channel_id=1, replica_groups=mesh['exp'=8,'tp'=4] {'exp'}, use_global_device_ids=true, to_apply=%region_35.36 | all-reduce | flops 1024 | bytes 4096 | tf_op jit(solution)/shard_map/psum | solution.py:302
  878.7 3.3 fusion.22
  882.0 40.7 %all-reduce.4 = (f32[2048]{0:T(1024)}, f32[2048]{0:T(1024)}) all-reduce(f32[2048]{0:T(1024)S(1)} %get-tuple-element.18, f32[2048]{0:T(1024)S(1)} %get-tuple-element.16), channel_id=1, replica_groups=mesh['exp'=8,'tp'=4] {'exp','tp'}, use_global_device_ids=true, to_apply=%region_29.30 | all-reduce | flops 4096 | bytes 32768 | tf_op jit(solution)/shard_map/psum | solution.py:305
  922.7 200.3 %all-reduce.12.cloned.1.call-done = (bf16[2048,512]{1,0:T(8,128)(2,1)}, bf16[2048,512]{1,0:T(8,128)(2,1)}, bf16[2048,512]{1,0:T(8,128)(2,1)}, bf16[512,2048]{1,0:T(8,128)(2,1)}) async-done(((bf16[2048,512]{1,0:T(8,128)(2,1)}, bf16[2048,512]{1,0:T(8,128)(2,1)}, bf16[2048,512]{1,0:T(8,128)(2,1)}, bf16[512,2048]{1,0:T(8,128)(2,1)}), (bf16[2048,512]{1,0:T(8,128)(2,1)}, bf16[2048,512]{1,0:T(8,128)(2,1)}, ...) | async-done | bytes 8388624 | tf_op jit(solution)/shard_map/psum | solution.py:298
  1123.0 4.3 convert_element_type.207
  1130.0 2.7 convert_element_type.211
  1135.3 115.1 %all-reduce.10.cloned.1.call-done = f32[2048,16]{0,1:T(8,128)} async-done(((f32[2048,16]{0,1:T(8,128)}), f32[2048,16]{0,1:T(8,128)}) %all-reduce.10.cloned.1.call-update) | async-done | bytes 131088 | tf_op jit(solution)/shard_map/psum | solution.py:305
  (269 shorter events, 79.8 us)
Async XLA Ops:
  7.2 382.3 %copy-start = (bf16[2,256,2048]{2,1,0:T(8,128)(2,1)S(1)}, bf16[2,256,2048]{2,1,0:T(8,128)(2,1)}, u32[]{:S(2)}) copy-start(bf16[2,256,2048]{2,1,0:T(8,128)(2,1)} %param.29) | copy-start | bytes 6291460
  7.2 29.5 %all-gather.5.cloned.1.call-start = ((), (), s32[]{:S(2)}) async-start(), calls=%async_computation.8 | async-start | bytes 2621440 | tf_op jit(solution)/shard_map/all_gather | solution.py:93
  11.2 82.1 %reduce-scatter.5.cloned.1.call-start = ((), (), s32[]{:S(2)}) async-start(), calls=%async_computation.9 | async-start | bytes 2621440 | tf_op jit(solution)/shard_map/reduce_scatter | solution.py:140
  15.7 34.2 %copy-start.31 = (f32[512,64]{1,0:T(8,128)}, f32[512,64]{1,0:T(8,128)S(1)}, u32[]{:S(2)}) copy-start(f32[512,64]{1,0:T(8,128)S(1)} %get-tuple-element.57) | copy-start | bytes 393220
  40.2 5.9 copy-start.23
  40.2 7.4 copy-start.52
  41.6 6.1 copy-start.62
  41.6 6.1 copy-start.64
  46.1 4.6 copy-start.54
  52.2 5.1 copy-start.2
  52.2 5.1 copy-start.57
  52.3 3.7 copy-start.71
  59.1 34.3 %copy-start.4 = (bf16[128,2048]{1,0:T(8,128)(2,1)S(1)}, bf16[128,2048]{1,0:T(8,128)(2,1)}, u32[]{:S(2)}) copy-start(bf16[128,2048]{1,0:T(8,128)(2,1)} %param.16) | copy-start | bytes 1572868
  59.1 35.6 %copy-start.50 = (f32[2048]{0:T(1024)S(1)}, f32[2048]{0:T(1024)}, u32[]{:S(2)}) copy-start(f32[2048]{0:T(1024)} %param.25) | copy-start | bytes 24580
  61.7 235.7 %all-gather.7.cloned.1.call-start = ((), (), s32[]{:S(2)}) async-start(), calls=%async_computation.10 | async-start | bytes 18350080 | tf_op jit(solution)/shard_map/all_gather | solution.py:61
  94.7 7.1 copy-start.66
  191.5 197.9 %all-gather.9.cloned.1.call-start = ((), (), s32[]{:S(2)}) async-start(), calls=%async_computation.12 | async-start | bytes 18350080 | tf_op jit(solution)/shard_map/all_gather | solution.py:198
  297.4 229.4 %reduce-scatter.7.cloned.1.call-start = ((), (), s32[]{:S(2)}) async-start(), calls=%async_computation.11 | async-start | bytes 18350080 | tf_op jit(solution)/shard_map/reduce_scatter | solution.py:178
  297.5 13.5 %copy-start.33 = (bf16[2,2048,256]{2,1,0:T(8,128)(2,1)S(1)}, bf16[2,2048,256]{2,1,0:T(8,128)(2,1)}, u32[]{:S(2)}) copy-start(bf16[2,2048,256]{2,1,0:T(8,128)(2,1)} %param.27) | copy-start | bytes 6291460
  413.8 228.5 %reduce-scatter.9.cloned.1.call-start = ((), (), s32[]{:S(2)}) async-start(), calls=%async_computation.13 | async-start | bytes 18350080 | tf_op jit(solution)/shard_map/reduce_scatter | solution.py:221
  415.3 19.2 %copy-start.35 = (bf16[2,2048,256]{2,1,0:T(8,128)(2,1)S(1)}, bf16[2,2048,256]{2,1,0:T(8,128)(2,1)}, u32[]{:S(2)}) copy-start(bf16[2,2048,256]{2,1,0:T(8,128)(2,1)} %param.28) | copy-start | bytes 6291460
  415.3 19.2 %copy-start.43 = (bf16[2,1792,256]{2,1,0:T(8,128)(2,1)S(1)}, bf16[2,1792,256]{2,1,0:T(8,128)(2,1)}, u32[]{:S(2)}) copy-start(bf16[2,1792,256]{2,1,0:T(8,128)(2,1)} %get-tuple-element.32) | copy-start | bytes 5505028
  534.4 115.5 %all-to-all-start.1 = ((bf16[2,448,2048]{2,0,1:T(2,128)(2,1)}), bf16[2,448,2048]{2,0,1:T(2,128)(2,1)}, u32[]{:S(2)}, u32[]{:S(2)}) async-start(bf16[2,448,2048]{2,0,1:T(2,128)(2,1)} %copy.151), calls=%async_computation.3 | async-start | bytes 7340032 | tf_op jit(solution)/shard_map/all_to_all | solution.py:181
  649.9 87.6 %all-to-all-start.3 = ((bf16[2,448,2048]{2,0,1:T(2,128)(2,1)}), bf16[2,448,2048]{2,0,1:T(2,128)(2,1)}, u32[]{:S(2)}, u32[]{:S(2)}) async-start(bf16[2,448,2048]{2,0,1:T(2,128)(2,1)} %copy.155), calls=%async_computation.6 | async-start | bytes 7340032 | tf_op jit(solution)/shard_map/all_to_all | solution.py:224
  655.4 127.8 %all-gather.11.cloned.1.call-start = ((), (), s32[]{:S(2)}) async-start(), calls=%async_computation.14 | async-start | bytes 2621440 | tf_op jit(solution)/shard_map/all_gather | solution.py:240
  754.8 5.2 copy-start.5
  754.8 5.2 copy-start.7
  754.8 5.2 copy-start.51
  754.8 5.2 copy-start.67
  754.8 6.3 copy-start.13
  762.3 114.9 %reduce-scatter.11.cloned.1.call-start = ((), (), s32[]{:S(2)}) async-start(), calls=%async_computation.15 | async-start | bytes 2621440 | tf_op jit(solution)/shard_map/reduce_scatter | solution.py:287
  783.2 3.7 copy-start.3
  797.4 5.2 copy-start.25
  804.2 3.6 copy-start.42
  812.4 310.6 %all-reduce.12.cloned.1.call-start = ((), (), s32[]{:S(2)}) async-start(), calls=%async_computation.17 | async-start | bytes 16777216 | tf_op jit(solution)/shard_map/psum | solution.py:298
  812.5 4.4 copy-start.72
  824.8 425.5 %all-reduce.10.cloned.1.call-start = ((), (), s32[]{:S(2)}) async-start(), calls=%async_computation.16 | async-start | bytes 262144 | tf_op jit(solution)/shard_map/psum | solution.py:305
  824.9 22.0 %slice-start = ((s8[14680064]{0:T(1024)(128)(4,1)}), s8[4194304]{0:T(1024)(128)(4,1)S(1)}, s32[]{:S(2)}) async-start(s8[14680064]{0:T(1024)(128)(4,1)} %bitcast.161), calls=%async_computation.18 | async-start | bytes 8388608
  824.9 22.0 %slice-start.1 = ((s8[14680064]{0:T(1024)(128)(4,1)}), s8[4194304]{0:T(1024)(128)(4,1)S(1)}, s32[]{:S(2)}) async-start(s8[14680064]{0:T(1024)(128)(4,1)} %bitcast.161), calls=%async_computation.19 | async-start | bytes 8388608
  835.9 11.0 copy-start.6
  835.9 11.0 slice-start.2
  835.9 11.1 slice-start.3
  847.0 5.7 copy-start.12
  847.0 30.2 %copy-start.56 = (f32[2048]{0:T(1024)S(1)}, f32[2048]{0:T(1024)}, u32[]{:S(2)}) copy-start(f32[2048]{0:T(1024)} %param.18) | copy-start | bytes 24580
  847.0 30.2 %copy-start.69 = (f32[128]{0:T(128)S(1)}, f32[128]{0:T(128)}, u32[]{:S(2)}) copy-start(f32[128]{0:T(128)} %copy-done.68) | copy-start | bytes 1540
  847.0 31.7 %copy-start.14 = (bf16[128,2048]{1,0:T(8,128)(2,1)S(1)}, bf16[128,2048]{1,0:T(8,128)(2,1)}, u32[]{:S(2)}) copy-start(bf16[128,2048]{1,0:T(8,128)(2,1)} %param.17) | copy-start | bytes 1572868
  1123.0 4.4 copy-start.40
  1130.0 121.9 %copy-start.1 = (bf16[2,256,2048]{2,1,0:T(8,128)(2,1)S(1)}, bf16[2,256,2048]{2,1,0:T(8,128)(2,1)}, u32[]{:S(2)}) copy-start(bf16[2,256,2048]{2,1,0:T(8,128)(2,1)} %param.29) | copy-start | bytes 6291460
  (43 other events, 85.5 us)
Sparse Core Ops, SparseCore 0:
  11.4 25.2 all-gather.4
  61.8 31.4 reduce-scatter.4
  191.6 92.0 all-gather.6
  297.5 91.9 all-gather.8
  413.9 112.8 reduce-scatter.6
  529.4 112.8 reduce-scatter.8
  762.4 20.6 all-gather.10
  812.5 31.4 reduce-scatter.10
  849.2 273.8 all-reduce.11
  1129.0 121.2 all-reduce.9
where the time goes:
time: 1270 us; the launch traced here: 1260 us
  waiting for transfers between devices  682 us (54%)
  blocking collectives  236 us (19%)
  matrix products  157 us (12%)
  local copies, waits for them, and re-layouts  97.1 us (8%)
  other arithmetic  58.7 us (5%)
  between operations  15.7 us (1%)
    psum x1, waiting for transfers between devices, body(): lax.psum(query_weight_grad.astype(jnp.bfloat16), 'exp').astype(jnp.float32)  200 us
    psum x1, waiting for transfers between devices, body(): lax.psum((attention_gain_grad, mixture_gain_grad, router_grad), ('exp', '...  115 us
    reduce_scatter x1, waiting for transfers between devices, body(): lax.psum_scatter(grad_in_part.astype(jnp.bfloat16), 'tp', scatter_dimensi...  102 us
    all_to_all x1, blocking collectives, body(): lax.all_to_all(outgoing, 'exp', split_axis=0, concat_axis=1, tiled=True)  87.5 us
    all_to_all x1, blocking collectives, body(): lax.all_to_all(grad_outgoing, 'exp', split_axis=0, concat_axis=1, tiled=T...  85 us
    reduce_scatter x1, waiting for transfers between devices, body(): lax.psum_scatter(partial_out.astype(jnp.bfloat16), 'tp', scatter_dimensio...  74.5 us
    all_gather x1, waiting for transfers between devices, body(): grad_expert = lax.all_gather(grad_arrived, 'tp', axis=1, tiled=True)  68.7 us
    all_to_all x1, waiting for transfers between devices, body(): lax.all_to_all(grad_in, 'exp', split_axis=1, concat_axis=0, tiled=True)  58.3 us
  transfers between devices with their start and end apart: 12, of which 9 were waited for; matrix products, arithmetic and copies ran while one was open for 15% of the time, Pallas kernels for 0%

commit v1 on v0

--- a/solution.py
+++ b/solution.py
@@ -295,7 +295,9 @@
         grad_attention_in * attention_gain, normed_one, scale_one
     )
     head_sums = (
-        lax.psum(query_weight_grad.astype(jnp.bfloat16), "exp").astype(jnp.float32),
+        jnp.sum(lax.all_gather(query_weight_grad.astype(jnp.bfloat16), "exp"), axis=0).astype(
+            jnp.float32
+        ),
         lax.psum(key_weight_grad.astype(jnp.bfloat16), "exp").astype(jnp.float32),
         lax.psum(value_weight_grad.astype(jnp.bfloat16), "exp").astype(jnp.float32),
         lax.psum(output_weight_grad.astype(jnp.bfloat16), "exp").astype(jnp.float32),

time: 1270 us -> 1440 us (1.13)
  waiting for transfers between devices: 682 us -> 837 us
    all_gather x0 -> x1, waiting for transfers between devices: none -> 220 us  [body(): lax.all_gather(query_weight_grad.astype(jnp.bfloat16), 'exp')]
    psum x1, waiting for transfers between devices: 200 us -> 138 us  [body(): lax.psum(key_weight_grad.astype(jnp.bfloat16), 'exp').astype(jnp.float32)]
  transfers between devices with their start and end apart: 12 -> 13, of which waited for: 9 -> 10; matrix products, arithmetic and copies ran while one was open for 15% -> 14% of each run, Pallas kernels for 0% -> 0%
where the time goes in v1:
time: 1440 us; the launch traced here: 1430 us
  waiting for transfers between devices  837 us (58%)
  blocking collectives  235 us (16%)
  matrix products  159 us (11%)
  local copies, waits for them, and re-layouts  98.1 us (7%)
  other arithmetic  70.9 us (5%)
  between operations  15.4 us (1%)
    all_gather x1, waiting for transfers between devices, body(): lax.all_gather(query_weight_grad.astype(jnp.bfloat16), 'exp')  220 us
    psum x1, waiting for transfers between devices, body(): lax.psum(key_weight_grad.astype(jnp.bfloat16), 'exp').astype(jnp.float32)  138 us
    psum x1, waiting for transfers between devices, body(): lax.psum((attention_gain_grad, mixture_gain_grad, router_grad), ('exp', '...  113 us
    reduce_scatter x1, waiting for transfers between devices, body(): lax.psum_scatter(grad_in_part.astype(jnp.bfloat16), 'tp', scatter_dimensi...  102 us
    all_to_all x1, blocking collectives, body(): lax.all_to_all(outgoing, 'exp', split_axis=0, concat_axis=1, tiled=True)  87.5 us
    all_to_all x1, blocking collectives, body(): lax.all_to_all(grad_outgoing, 'exp', split_axis=0, concat_axis=1, tiled=T...  85 us
    reduce_scatter x1, waiting for transfers between devices, body(): lax.psum_scatter(partial_out.astype(jnp.bfloat16), 'tp', scatter_dimensio...  74.5 us
    all_gather x1, waiting for transfers between devices, body(): grad_expert = lax.all_gather(grad_arrived, 'tp', axis=1, tiled=True)  68.7 us
  transfers between devices with their start and end apart: 13, of which 10 were waited for; matrix products, arithmetic and copies ran while one was open for 14% of the time, Pallas kernels for 0%

profile of v1, /device:TPU:0, one launch (start us, length us, event | category | flops | bytes accessed | tf_op | source)
XLA Modules:
  0.0 1429.0 jit_solution(8788435941878631585)
XLA Ops:
  15.8 21.0 %all-gather.7.cloned.1.call-done = bf16[512,2048]{1,0:T(8,128)(2,1)} async-done(((bf16[128,2048]{1,0:T(8,128)(2,1)}), bf16[512,2048]{1,0:T(8,128)(2,1)}) %all-gather.7.cloned.1.call-update) | async-done | bytes 2097168 | tf_op jit(solution)/shard_map/all_gather | solution.py:93
  36.7 3.5 multiply_reduce_fusion.6
  41.6 4.5 multiply_reduce_fusion.7
  62.5 4.5 reduce-window.6
  67.5 4.3 scatter_custom_fusion
  71.9 21.5 %reduce-scatter.5.cloned.1.call-done = bf16[128,2048]{1,0:T(8,128)(2,1)} async-done(((bf16[512,2048]{1,0:T(8,128)(2,1)}), bf16[128,2048]{1,0:T(8,128)(2,1)}) %reduce-scatter.5.cloned.1.call-update) | async-done | bytes 524304 | tf_op jit(solution)/shard_map/reduce_scatter | solution.py:140
  96.8 5.0 gather_fusion
  101.8 87.5 %all_to_all.66 = bf16[16,56,2048]{2,1,0:T(8,128)(2,1)S(1)} all-to-all(bf16[16,56,2048]{2,1,0:T(8,128)(2,1)} %bitcast.165), channel_id=1, replica_groups=mesh['exp'=8,'tp'=4] {'exp'}, dimensions={0} | all-to-all | bytes 7340032 | tf_op jit(solution)/shard_map/all_to_all | solution.py:168
  197.7 12.3 gather_fusion.2
  210.1 85.0 %all_to_all.67 = bf16[16,56,2048]{2,1,0:T(8,128)(2,1)S(1)} all-to-all(bf16[16,56,2048]{2,1,0:T(8,128)(2,1)} %bitcast.166), channel_id=1, replica_groups=mesh['exp'=8,'tp'=4] {'exp'}, dimensions={0} | all-to-all | bytes 7340032 | tf_op jit(solution)/shard_map/all_to_all | solution.py:197
  297.5 13.5 fusion.53
  311.0 9.8 fusion.52
  320.8 68.7 %all-gather.11.cloned.1.call-done = bf16[2,1792,2048]{2,1,0:T(8,128)(2,1)} async-done(((bf16[2,448,2048]{2,1,0:T(8,128)(2,1)}), bf16[2,1792,2048]{2,1,0:T(8,128)(2,1)}) %all-gather.11.cloned.1.call-update) | async-done | bytes 14680080 | tf_op jit(solution)/shard_map/all_gather | solution.py:198
  389.5 15.6 %multiply_convert_fusion.1 = (bf16[2,1792,256]{2,1,0:T(8,128)(2,1)}, bf16[2,1792,256]{2,1,0:T(8,128)(2,1)}, bf16[2,1792,256]{2,1,0:T(8,128)(2,1)}) fusion(f32[2,1792,256]{2,1,0:T(8,128)} %fusion.52, f32[2,1792,256]{2,1,0:T(8,128)} %fusion.53, bf16[2,1792,2048]{2,1,0:T(8,128)(2,1)} %all-gather.11.cloned.1.call-done, bf16[2,256,2048]{2,1,0:T(8,128)(2,1)S(1)} %copy-done), kind=kOutput, calls=%fused_computation.22 | convolution fusion | flops 3771858944 | bytes 29622272 | tf_op jit(solution)/shard_map/erd,efd->erf/dot_general | solution.py:206
  405.0 8.8 convolution_convert_fusion
  415.4 19.2 %fusion.54 = f32[2,1792,2048]{2,1,0:T(8,128)} fusion(bf16[2,1792,256]{2,1,0:T(8,128)(2,1)} %get-tuple-element.32, bf16[2,2048,256]{2,1,0:T(8,128)(2,1)S(1)} %copy-done.34), kind=kOutput, calls=%fused_computation.160 | convolution fusion | flops 3758096384 | bytes 33292288 | tf_op jit(solution)/shard_map/erf,edf->erd/dot_general | solution.py:218
  434.6 17.7 %add_convert_fusion = bf16[2,1792,2048]{2,1,0:T(8,128)(2,1)} fusion(f32[2,1792,2048]{2,1,0:T(8,128)} %fusion.54, bf16[2,1792,256]{2,1,0:T(8,128)(2,1)S(1)} %copy-done.42, bf16[2,2048,256]{2,1,0:T(8,128)(2,1)S(1)} %copy-done.35), kind=kOutput, calls=%fused_computation.5 | convolution fusion | flops 3772776448 | bytes 47972352 | tf_op jit(solution)/shard_map/erf,edf->erd/dot_general | solution.py:220
  452.3 74.5 %reduce-scatter.7.cloned.1.call-done = bf16[2,448,2048]{2,1,0:T(8,128)(2,1)} async-done(((bf16[2,1792,2048]{2,1,0:T(8,128)(2,1)}), bf16[2,448,2048]{2,1,0:T(8,128)(2,1)}) %reduce-scatter.7.cloned.1.call-update) | async-done | bytes 3670032 | tf_op jit(solution)/shard_map/reduce_scatter | solution.py:178
  526.8 7.6 copy.151
  534.4 5.5 all-to-all-start.1
  539.9 102.3 %reduce-scatter.9.cloned.1.call-done = bf16[2,448,2048]{2,1,0:T(8,128)(2,1)} async-done(((bf16[2,1792,2048]{2,1,0:T(8,128)(2,1)}), bf16[2,448,2048]{2,1,0:T(8,128)(2,1)}) %reduce-scatter.9.cloned.1.call-update) | async-done | bytes 3670032 | tf_op jit(solution)/shard_map/reduce_scatter | solution.py:221
  642.3 7.6 copy.155
  649.9 5.5 all-to-all-start.3
  655.9 3.7 copy.152
  661.9 11.3 gather_fusion.1
  673.2 5.9 fusion.1
  679.2 58.3 %all-to-all-done.3 = bf16[2,448,2048]{2,0,1:T(2,128)(2,1)} async-done(((bf16[2,448,2048]{2,0,1:T(2,128)(2,1)}), bf16[2,448,2048]{2,0,1:T(2,128)(2,1)}, u32[]{:S(2)}, u32[]{:S(2)}) %all-to-all-start.3) | async-done | bytes 3670048 | tf_op jit(solution)/shard_map/all_to_all | solution.py:224
  737.5 3.7 copy.156
  743.5 11.3 gather_fusion.3
  754.8 5.2 convert_reduce_fusion
  762.6 20.6 %all-gather.13.cloned.1.call-done = bf16[512,2048]{1,0:T(8,128)(2,1)} async-done(((bf16[128,2048]{1,0:T(8,128)(2,1)}), bf16[512,2048]{1,0:T(8,128)(2,1)}) %all-gather.13.cloned.1.call-update) | async-done | bytes 2097168 | tf_op jit(solution)/shard_map/all_gather | solution.py:240
  783.2 3.6 convolution_convert_fusion.6
  804.3 3.1 fusion.55
  809.7 2.7 add_convert_fusion.1
  812.5 4.4 convolution_convert_fusion.1
  823.2 4.2 convolution_convert_fusion.4
  827.5 11.3 fusion.58
  838.9 11.0 fusion.57
  850.0 5.7 fusion.59
  856.7 22.3 %all-reduce.5 = (bf16[512]{0:T(512)(128)(2,1)S(1)}, bf16[512]{0:T(512)(128)(2,1)S(1)}) all-reduce(bf16[512]{0:T(512)(128)(2,1)S(1)} %get-tuple-element.36, bf16[512]{0:T(512)(128)(2,1)S(1)} %get-tuple-element.34), channel_id=1, replica_groups=mesh['exp'=8,'tp'=4] {'exp'}, use_global_device_ids=true, to_apply=%region_35.36 | all-reduce | flops 1024 | bytes 4096 | tf_op jit(solution)/shard_map/psum | solution.py:304
  881.7 3.3 fusion.22
  885.0 40.7 %all-reduce.4 = (f32[2048]{0:T(1024)}, f32[2048]{0:T(1024)}) all-reduce(f32[2048]{0:T(1024)S(1)} %get-tuple-element.18, f32[2048]{0:T(1024)S(1)} %get-tuple-element.16), channel_id=1, replica_groups=mesh['exp'=8,'tp'=4] {'exp','tp'}, use_global_device_ids=true, to_apply=%region_29.30 | all-reduce | flops 4096 | bytes 32768 | tf_op jit(solution)/shard_map/psum | solution.py:307
  925.6 137.9 %all-reduce.12.cloned.1.call-done = (bf16[2048,512]{1,0:T(8,128)(2,1)}, bf16[2048,512]{1,0:T(8,128)(2,1)}, bf16[512,2048]{1,0:T(8,128)(2,1)}) async-done(((bf16[2048,512]{1,0:T(8,128)(2,1)}, bf16[2048,512]{1,0:T(8,128)(2,1)}, bf16[512,2048]{1,0:T(8,128)(2,1)}), (bf16[2048,512]{1,0:T(8,128)(2,1)}, bf16[2048,512]{1,0:T(8,128)(2,1)}, bf16[512,2048]{1,0:T(8,128)(2,1)})) %all-reduce.12.cloned.1.call-update) | async-done | bytes 6291472 | tf_op jit(solution)/shard_map/psum | solution.py:301
  1063.5 4.3 convert_element_type.211
  1073.0 219.8 %all-gather.15.cloned.1.call-done = bf16[16384,512]{1,0:T(8,128)(2,1)} async-done(((bf16[2048,512]{1,0:T(8,128)(2,1)}), bf16[16384,512]{1,0:T(8,128)(2,1)}) %all-gather.15.cloned.1.call-update) | async-done | bytes 16777232 | tf_op jit(solution)/shard_map/all_gather | solution.py:298
  1292.9 10.7 reduce_sum.239
  1303.6 4.2 convert_element_type.209
  1307.8 112.8 %all-reduce.10.cloned.1.call-done = f32[2048,16]{0,1:T(8,128)} async-done(((f32[2048,16]{0,1:T(8,128)}), f32[2048,16]{0,1:T(8,128)}) %all-reduce.10.cloned.1.call-update) | async-done | bytes 131088 | tf_op jit(solution)/shard_map/psum | solution.py:307
  (271 shorter events, 86.2 us)
Async XLA Ops:
  7.2 382.3 %copy-start = (bf16[2,256,2048]{2,1,0:T(8,128)(2,1)S(1)}, bf16[2,256,2048]{2,1,0:T(8,128)(2,1)}, u32[]{:S(2)}) copy-start(bf16[2,256,2048]{2,1,0:T(8,128)(2,1)} %param.29) | copy-start | bytes 6291460
  7.2 29.5 %all-gather.7.cloned.1.call-start = ((), (), s32[]{:S(2)}) async-start(), calls=%async_computation.8 | async-start | bytes 2621440 | tf_op jit(solution)/shard_map/all_gather | solution.py:93
  11.3 82.1 %reduce-scatter.5.cloned.1.call-start = ((), (), s32[]{:S(2)}) async-start(), calls=%async_computation.9 | async-start | bytes 2621440 | tf_op jit(solution)/shard_map/reduce_scatter | solution.py:140
  15.8 34.2 %copy-start.31 = (f32[512,64]{1,0:T(8,128)}, f32[512,64]{1,0:T(8,128)S(1)}, u32[]{:S(2)}) copy-start(f32[512,64]{1,0:T(8,128)S(1)} %get-tuple-element.56) | copy-start | bytes 393220
  40.2 5.9 copy-start.23
  40.3 7.4 copy-start.51
  41.6 6.1 copy-start.61
  41.6 6.1 copy-start.63
  46.1 4.6 copy-start.53
  52.2 5.1 copy-start.2
  52.2 5.1 copy-start.56
  52.3 3.7 copy-start.70
  59.1 34.3 %copy-start.4 = (bf16[128,2048]{1,0:T(8,128)(2,1)S(1)}, bf16[128,2048]{1,0:T(8,128)(2,1)}, u32[]{:S(2)}) copy-start(bf16[128,2048]{1,0:T(8,128)(2,1)} %param.16) | copy-start | bytes 1572868
  59.1 35.6 %copy-start.49 = (f32[2048]{0:T(1024)S(1)}, f32[2048]{0:T(1024)}, u32[]{:S(2)}) copy-start(f32[2048]{0:T(1024)} %param.25) | copy-start | bytes 24580
  61.7 235.7 %all-gather.9.cloned.1.call-start = ((), (), s32[]{:S(2)}) async-start(), calls=%async_computation.10 | async-start | bytes 18350080 | tf_op jit(solution)/shard_map/all_gather | solution.py:61
  94.7 7.1 copy-start.65
  191.5 197.9 %all-gather.11.cloned.1.call-start = ((), (), s32[]{:S(2)}) async-start(), calls=%async_computation.12 | async-start | bytes 18350080 | tf_op jit(solution)/shard_map/all_gather | solution.py:198
  297.4 229.4 %reduce-scatter.7.cloned.1.call-start = ((), (), s32[]{:S(2)}) async-start(), calls=%async_computation.11 | async-start | bytes 18350080 | tf_op jit(solution)/shard_map/reduce_scatter | solution.py:178
  297.5 13.5 copy-start.33
  413.8 228.5 %reduce-scatter.9.cloned.1.call-start = ((), (), s32[]{:S(2)}) async-start(), calls=%async_computation.13 | async-start | bytes 18350080 | tf_op jit(solution)/shard_map/reduce_scatter | solution.py:221
  415.4 19.2 %copy-start.35 = (bf16[2,2048,256]{2,1,0:T(8,128)(2,1)S(1)}, bf16[2,2048,256]{2,1,0:T(8,128)(2,1)}, u32[]{:S(2)}) copy-start(bf16[2,2048,256]{2,1,0:T(8,128)(2,1)} %param.28) | copy-start | bytes 6291460
  415.4 19.2 %copy-start.42 = (bf16[2,1792,256]{2,1,0:T(8,128)(2,1)S(1)}, bf16[2,1792,256]{2,1,0:T(8,128)(2,1)}, u32[]{:S(2)}) copy-start(bf16[2,1792,256]{2,1,0:T(8,128)(2,1)} %get-tuple-element.31) | copy-start | bytes 5505028
  534.4 115.5 %all-to-all-start.1 = ((bf16[2,448,2048]{2,0,1:T(2,128)(2,1)}), bf16[2,448,2048]{2,0,1:T(2,128)(2,1)}, u32[]{:S(2)}, u32[]{:S(2)}) async-start(bf16[2,448,2048]{2,0,1:T(2,128)(2,1)} %copy.151), calls=%async_computation.3 | async-start | bytes 7340032 | tf_op jit(solution)/shard_map/all_to_all | solution.py:181
  649.9 87.6 %all-to-all-start.3 = ((bf16[2,448,2048]{2,0,1:T(2,128)(2,1)}), bf16[2,448,2048]{2,0,1:T(2,128)(2,1)}, u32[]{:S(2)}, u32[]{:S(2)}) async-start(bf16[2,448,2048]{2,0,1:T(2,128)(2,1)} %copy.155), calls=%async_computation.6 | async-start | bytes 7340032 | tf_op jit(solution)/shard_map/all_to_all | solution.py:224
  655.4 127.8 %all-gather.13.cloned.1.call-start = ((), (), s32[]{:S(2)}) async-start(), calls=%async_computation.14 | async-start | bytes 2621440 | tf_op jit(solution)/shard_map/all_gather | solution.py:240
  754.8 5.2 copy-start.5
  754.8 5.2 copy-start.7
  754.8 5.2 copy-start.50
  754.8 5.2 copy-start.66
  754.8 6.3 copy-start.13
  762.3 117.8 %reduce-scatter.11.cloned.1.call-start = ((), (), s32[]{:S(2)}) async-start(), calls=%async_computation.15 | async-start | bytes 2621440 | tf_op jit(solution)/shard_map/reduce_scatter | solution.py:287
  783.2 3.7 copy-start.3
  797.5 5.2 copy-start.25
  812.4 251.1 %all-reduce.12.cloned.1.call-start = ((), (), s32[]{:S(2)}) async-start(), calls=%async_computation.18 | async-start | bytes 12582912 | tf_op jit(solution)/shard_map/psum | solution.py:301
  812.5 4.4 copy-start.71
  822.2 470.7 %all-gather.15.cloned.1.call-start = ((), (), s32[]{:S(2)}) async-start(), calls=%async_computation.17 | async-start | bytes 18874368 | tf_op jit(solution)/shard_map/all_gather | solution.py:298
  827.5 593.1 %all-reduce.10.cloned.1.call-start = ((), (), s32[]{:S(2)}) async-start(), calls=%async_computation.16 | async-start | bytes 262144 | tf_op jit(solution)/shard_map/psum | solution.py:307
  827.5 22.4 %slice-start = ((s8[14680064]{0:T(1024)(128)(4,1)}), s8[4194304]{0:T(1024)(128)(4,1)S(1)}, s32[]{:S(2)}) async-start(s8[14680064]{0:T(1024)(128)(4,1)} %bitcast.162), calls=%async_computation.19 | async-start | bytes 8388608
  827.5 22.4 %slice-start.1 = ((s8[14680064]{0:T(1024)(128)(4,1)}), s8[4194304]{0:T(1024)(128)(4,1)S(1)}, s32[]{:S(2)}) async-start(s8[14680064]{0:T(1024)(128)(4,1)} %bitcast.162), calls=%async_computation.20 | async-start | bytes 8388608
  838.9 11.0 copy-start.6
  838.9 11.0 slice-start.2
  838.9 11.1 slice-start.3
  850.0 5.7 copy-start.12
  850.0 30.2 %copy-start.55 = (f32[2048]{0:T(1024)S(1)}, f32[2048]{0:T(1024)}, u32[]{:S(2)}) copy-start(f32[2048]{0:T(1024)} %param.18) | copy-start | bytes 24580
  850.0 30.2 %copy-start.68 = (f32[128]{0:T(128)S(1)}, f32[128]{0:T(128)}, u32[]{:S(2)}) copy-start(f32[128]{0:T(128)} %copy-done.67) | copy-start | bytes 1540
  850.0 31.7 %copy-start.14 = (bf16[128,2048]{1,0:T(8,128)(2,1)S(1)}, bf16[128,2048]{1,0:T(8,128)(2,1)}, u32[]{:S(2)}) copy-start(bf16[128,2048]{1,0:T(8,128)(2,1)} %param.17) | copy-start | bytes 1572868
  1063.5 4.4 copy-start.39
  1292.9 129.2 %copy-start.1 = (bf16[2,256,2048]{2,1,0:T(8,128)(2,1)S(1)}, bf16[2,256,2048]{2,1,0:T(8,128)(2,1)}, u32[]{:S(2)}) copy-start(bf16[2,256,2048]{2,1,0:T(8,128)(2,1)} %param.29) | copy-start | bytes 6291460
  (43 other events, 84.7 us)
Sparse Core Ops, SparseCore 0:
  11.4 25.2 all-gather.6
  61.9 31.4 reduce-scatter.4
  191.7 92.0 all-gather.8
  297.5 91.9 all-gather.10
  413.9 112.8 reduce-scatter.6
  529.4 112.8 reduce-scatter.8
  762.5 20.7 all-gather.12
  812.6 31.4 reduce-scatter.10
  848.9 214.5 all-reduce.11
  1066.3 226.5 all-gather.14
  1299.9 120.5 all-reduce.9
